TPU v7x, 1024 devices: a whole 4x8x16 slice. The times are simulated.
1024 devices in a mesh: section: 16 (over x, z_hi), expert: 64 (over y, z_lo, core).
Axes of the slice: x: 4, y: 8, z: 16 (z_hi: 4, z_lo: 4; z = z_hi * 4 + z_lo), core: 2. Of those that a mesh axis runs over, the one named last changes fastest.
Arguments:
- tokens_a: bfloat16 [1024, 3584], P('expert'), may hold values from -6 to 6
- routes_a: int32 [1024, 8], P('expert'), may hold values from 0 to 63, as said below
- gates_a: float32 [1024, 8], P('expert'), may hold values from 0.1 to 0.4
- cotangent_b: bfloat16 [1024, 3584], P('expert'), may hold values from -6 to 6
- routes_b: int32 [1024, 8], P('expert'), may hold values from 0 to 63, as said below
- gates_b: float32 [1024, 8], P('expert'), may hold values from 0.1 to 0.4
- gate_weight: bfloat16 [64, 3584, 2048], P('expert', None, 'section'), may hold values from -0.09375 to 0.09375
- up_weight: bfloat16 [64, 3584, 2048], P('expert', None, 'section'), may hold values from -0.09375 to 0.09375
- down_weight: bfloat16 [64, 2048, 3584], P('expert', 'section'), may hold values from -0.125 to 0.125
- saved_gate: bfloat16 [64, 192, 2048], P('expert', None, 'section'), may hold values from -6 to 6
- saved_up: bfloat16 [64, 192, 2048], P('expert', None, 'section'), may hold values from -6 to 6
Outputs:
- forward_out: bfloat16 [1024, 3584], P('expert', 'section')
- input_grad: bfloat16 [1024, 3584], P('expert', 'section')
Inputs may be any that keep to these rules, and one draw needn't show every extreme that they name: `routes_a`: each row names 8 different experts. Within each aligned block of 16 rows no expert is named more than 3 times, and one expert, the same in every block, is named exactly 3 times in each block. `routes_b`: each row names 8 different experts. Within each aligned block of 16 rows no expert is named more than 3 times, and one expert, the same in every block, is named exactly 3 times in each block.
All inputs are finite; a program needn't handle non-finite values.
Results may differ from a plain program's by a relative error of at most 0.015.
Values may be sent and summed in bfloat16 or wider, within the bound.
A program may use at most 32 MiB of HBM per device.

v0:
```python
import jax
import jax.numpy as jnp
from jax import lax
from jax.sharding import PartitionSpec as P


def route_slots(routes, experts, capacity):
    flat_ids = routes.reshape(-1)
    onehot = (flat_ids[:, None] == jnp.arange(experts, dtype=jnp.int32)[None, :]).astype(jnp.int32)
    before = jnp.cumsum(onehot, axis=0) - onehot
    ranking = jnp.sum(before * onehot, axis=1)
    return flat_ids * capacity + ranking


def fill_slots(values, slot_index, slot_total):
    return jnp.zeros((slot_total, values.shape[1]), values.dtype).at[slot_index].set(values)


def body(
    tokens_a,
    routes_a,
    gates_a,
    cotangent_b,
    routes_b,
    gates_b,
    gate_weight,
    up_weight,
    down_weight,
    saved_gate,
    saved_up,
):
    experts = lax.axis_size("expert")
    sections = lax.axis_size("section")
    token_count, feature_count = tokens_a.shape
    top_count = routes_a.shape[1]
    slot_count = saved_gate.shape[1]
    capacity = slot_count // experts
    column_count = feature_count // sections
    where_a = route_slots(routes_a, experts, capacity)
    where_b = route_slots(routes_b, experts, capacity)
    values_a = jnp.repeat(tokens_a, top_count, axis=0)
    repeated_b = jnp.repeat(cotangent_b, top_count, axis=0)
    gate_col = gates_b.reshape(-1, 1)
    values_b = (gate_col * repeated_b.astype(jnp.float32)).astype(jnp.bfloat16)
    send_a = fill_slots(values_a, where_a, slot_count).reshape(experts, capacity, feature_count)
    recv_a = lax.all_to_all(send_a, "expert", split_axis=0, concat_axis=0, tiled=True)
    send_b = fill_slots(values_b, where_b, slot_count).reshape(experts, capacity, feature_count)
    recv_b = lax.all_to_all(send_b, "expert", split_axis=0, concat_axis=0, tiled=True)
    rows_a = recv_a.reshape(slot_count, feature_count)
    rows_b = recv_b.reshape(slot_count, feature_count)
    w_gate = gate_weight[0]
    w_up = up_weight[0]
    w_down = down_weight[0]
    gate_pre = jnp.dot(rows_a, w_gate, preferred_element_type=jnp.float32)
    up_pre = jnp.dot(rows_a, w_up, preferred_element_type=jnp.float32)
    hidden = (jax.nn.silu(gate_pre) * up_pre).astype(jnp.bfloat16)
    part_y = jnp.dot(hidden, w_down, preferred_element_type=jnp.float32)
    grad_hidden = lax.dot_general(
        rows_b, w_down, (((1,), (1,)), ((), ())), preferred_element_type=jnp.float32
    )
    pre_gate = saved_gate[0].astype(jnp.float32)
    pre_up = saved_up[0].astype(jnp.float32)
    squash = jax.nn.sigmoid(pre_gate)
    grad_up = (grad_hidden * (pre_gate * squash)).astype(jnp.bfloat16)
    grad_gate = (grad_hidden * pre_up * squash * (1.0 + pre_gate * (1.0 - squash))).astype(
        jnp.bfloat16
    )
    contract = (((1,), (1,)), ((), ()))
    part_dx = lax.dot_general(grad_gate, w_gate, contract, preferred_element_type=jnp.float32)
    part_dx = part_dx + lax.dot_general(grad_up, w_up, contract, preferred_element_type=jnp.float32)
    summed_y, summed_dx = (
        lax.psum_scatter(
            part_y.astype(jnp.bfloat16), "section", scatter_dimension=1, tiled=True
        ).astype(jnp.float32),
        lax.psum_scatter(
            part_dx.astype(jnp.bfloat16), "section", scatter_dimension=1, tiled=True
        ).astype(jnp.float32),
    )
    out_y = summed_y.astype(jnp.bfloat16).reshape(experts, capacity, column_count)
    out_dx = summed_dx.astype(jnp.bfloat16).reshape(experts, capacity, column_count)
    back_y, back_dx = (
        lax.all_to_all(out_y, "expert", split_axis=0, concat_axis=0, tiled=True),
        lax.all_to_all(out_dx, "expert", split_axis=0, concat_axis=0, tiled=True),
    )
    returned_y = back_y.reshape(slot_count, column_count)[where_a].reshape(
        token_count, top_count, column_count
    )
    returned_dx = back_dx.reshape(slot_count, column_count)[where_b].reshape(
        token_count, top_count, column_count
    )
    forward_out = jnp.sum(gates_a[:, :, None] * returned_y.astype(jnp.float32), axis=1).astype(
        jnp.bfloat16
    )
    input_grad = jnp.sum(returned_dx.astype(jnp.float32), axis=1).astype(jnp.bfloat16)
    return (forward_out, input_grad)


def solution(mesh):
    placed = (
        P("expert", None),
        P("expert", None),
        P("expert", None),
        P("expert", None),
        P("expert", None),
        P("expert", None),
        P("expert", None, "section"),
        P("expert", None, "section"),
        P("expert", "section", None),
        P("expert", None, "section"),
        P("expert", None, "section"),
    )
    return jax.shard_map(
        body,
        mesh=mesh,
        in_specs=placed,
        out_specs=(P("expert", "section"), P("expert", "section")),
        check_vma=False,
    )
```

profile of v0, /device:TPU:1, one launch (start us, length us, event | category | flops | bytes accessed | tf_op | source)
XLA Modules:
  0.0 377.3 jit_solution(3856880486868002051)
XLA Ops:
  7.2 0.0 copy-start
  7.2 0.8 copy.29
  8.0 0.7 broadcast_multiply_fusion
  8.7 0.1 eq.34
  8.8 0.1 fusion.37
  8.9 0.2 reduce_window_sum.18
  9.1 0.2 select_reduce_fusion
  9.2 0.1 copy.28
  9.3 0.1 mul.83
  9.4 0.9 convert_element_type.65
  10.3 0.8 copy.30
  11.1 0.1 mul.85
  11.2 2.3 scatter_custom_fusion.1
  13.6 2.1 reshape.111
  15.7 18.4 %all-to-all-start.2 = ((bf16[64,3,3584]{2,1,0:T(4,128)(2,1)}), bf16[64,3,3584]{2,1,0:T(4,128)(2,1)S(1)}, u32[]{:S(2)}, u32[]{:S(2)}) async-start(bf16[64,3,3584]{2,1,0:T(4,128)(2,1)} %reshape.111), calls=%async_computation.2 | async-start | bytes 3670016 | tf_op jit(solution)/shard_map/all_to_all | solution.py:48
  34.1 0.0 copy-done.5
  34.1 0.1 copy.27
  34.1 0.1 eq.30
  34.2 0.1 fusion.38
  34.3 0.2 reduce_window_sum.17
  34.5 0.1 copy.26
  34.6 0.1 mul.77
  34.7 0.2 select_reduce_fusion.1
  34.9 0.0 copy-done.3
  34.9 3.1 scatter_custom_fusion
  37.9 3.9 %reshape.107 = bf16[64,3,3584]{2,1,0:T(4,128)(2,1)} reshape(bf16[192,3584]{1,0:T(8,128)(2,1)} %scatter_custom_fusion) | data formatting | bytes 2752512 | tf_op jit(solution)/shard_map/reshape | solution.py:45
  41.9 36.2 %all-to-all-done.2 = bf16[64,3,3584]{2,1,0:T(4,128)(2,1)S(1)} async-done(((bf16[64,3,3584]{2,1,0:T(4,128)(2,1)}), bf16[64,3,3584]{2,1,0:T(4,128)(2,1)S(1)}, u32[]{:S(2)}, u32[]{:S(2)}) %all-to-all-start.2) | async-done | bytes 1376288 | tf_op jit(solution)/shard_map/all_to_all | solution.py:48
  78.1 7.6 %all-to-all-start = ((bf16[64,3,3584]{2,1,0:T(4,128)(2,1)}), bf16[64,3,3584]{2,1,0:T(4,128)(2,1)}, u32[]{:S(2)}, u32[]{:S(2)}) async-start(bf16[64,3,3584]{2,1,0:T(4,128)(2,1)} %reshape.107), calls=%async_computation | async-start | bytes 3670016 | tf_op jit(solution)/shard_map/all_to_all | solution.py:46
  85.7 0.0 reduce-scatter.9.cloned.1.call-start
  85.8 2.4 reshape.112
  88.2 2.2 fusion.5
  90.3 0.0 copy-done.1
  90.4 0.0 copy-done.2
  90.4 0.0 copy-done.4
  90.4 0.5 fusion.11
  90.9 0.0 copy-done
  90.9 0.5 fusion
  91.5 2.3 copy.33
  93.7 0.0 reduce-scatter.9.cloned.1.call-update
  93.8 0.0 reduce-scatter.7.cloned.1.call-start
  93.8 40.7 %all-to-all-done = bf16[64,3,3584]{2,1,0:T(4,128)(2,1)} async-done(((bf16[64,3,3584]{2,1,0:T(4,128)(2,1)}), bf16[64,3,3584]{2,1,0:T(4,128)(2,1)}, u32[]{:S(2)}, u32[]{:S(2)}) %all-to-all-start) | async-done | bytes 1376288 | tf_op jit(solution)/shard_map/all_to_all | solution.py:46
  134.5 3.0 reshape.108
  137.5 0.5 fusion.13
  138.0 3.2 convolution_convert_fusion
  141.2 3.6 copy.31
  144.8 0.0 reduce-scatter.7.cloned.1.call-update
  144.9 75.4 %reduce-scatter.9.cloned.1.call-done = bf16[224,192]{1,0:T(8,128)(2,1)} async-done(((bf16[3584,192]{1,0:T(8,128)(2,1)}), bf16[224,192]{1,0:T(8,128)(2,1)}) %reduce-scatter.9.cloned.1.call-update) | async-done | bytes 86032
  220.3 1.0 copy.34
  221.3 0.7 reshape.113
  222.0 9.8 %all-to-all-start.3 = ((bf16[64,3,224]{2,1,0:T(4,128)(2,1)}), bf16[64,3,224]{2,1,0:T(4,128)(2,1)S(1)}, u32[]{:S(2)}, u32[]{:S(2)}) async-start(bf16[64,3,224]{2,1,0:T(4,128)(2,1)} %reshape.113), calls=%async_computation.3 | async-start | bytes 262144 | tf_op jit(solution)/shard_map/all_to_all | solution.py:83
  231.8 0.0 copy-done.6
  231.8 0.1 copy.25
  231.9 114.6 %reduce-scatter.7.cloned.1.call-done = bf16[224,192]{1,0:T(8,128)(2,1)} async-done(((bf16[3584,192]{1,0:T(8,128)(2,1)}), bf16[224,192]{1,0:T(8,128)(2,1)}) %reduce-scatter.7.cloned.1.call-update) | async-done | bytes 86032
  346.5 1.0 copy.32
  347.5 0.7 reshape.109
  348.2 0.0 all-to-all-done.3
  348.2 9.8 %all-to-all-start.1 = ((bf16[64,3,224]{2,1,0:T(4,128)(2,1)}), bf16[64,3,224]{2,1,0:T(4,128)(2,1)S(1)}, u32[]{:S(2)}, u32[]{:S(2)}) async-start(bf16[64,3,224]{2,1,0:T(4,128)(2,1)} %reshape.109), calls=%async_computation.1 | async-start | bytes 262144 | tf_op jit(solution)/shard_map/all_to_all | solution.py:82
  358.0 0.1 reshape.114
  358.1 0.8 gather_fusion.1
  359.0 0.6 bitcast_reduce_fusion
  359.6 9.2 %all-to-all-done.1 = bf16[64,3,224]{2,1,0:T(4,128)(2,1)S(1)} async-done(((bf16[64,3,224]{2,1,0:T(4,128)(2,1)}), bf16[64,3,224]{2,1,0:T(4,128)(2,1)S(1)}, u32[]{:S(2)}, u32[]{:S(2)}) %all-to-all-start.1) | async-done | bytes 86048 | tf_op jit(solution)/shard_map/all_to_all | solution.py:82
  368.8 0.1 reshape.110
  368.9 0.8 gather_fusion
  369.8 0.7 fusion.22
  (11 shorter events, 0.0 us)
Async XLA Ops:
  7.2 83.7 %copy-start = (bf16[1,3584,128]{2,1,0:T(8,128)(2,1)S(1)}, bf16[1,3584,128]{2,1,0:T(8,128)(2,1)}, u32[]{:S(2)}) copy-start(bf16[1,3584,128]{2,1,0:T(8,128)(2,1)} %param.18) | copy-start | bytes 2752516
  15.7 18.4 %copy-start.5 = (s32[16,8]{0,1:T(8,128)S(1)}, s32[16,8]{0,1:T(8,128)}, u32[]{:S(2)}) copy-start(s32[16,8]{0,1:T(8,128)} %param.12) | copy-start | bytes 1540
  15.7 19.2 %copy-start.3 = (bf16[16,3584]{1,0:T(8,128)(2,1)S(1)}, bf16[16,3584]{1,0:T(8,128)(2,1)}, u32[]{:S(2)}) copy-start(bf16[16,3584]{1,0:T(8,128)(2,1)} %param.11) | copy-start | bytes 344068
  15.7 62.4 %all-to-all-start.2 = ((bf16[64,3,3584]{2,1,0:T(4,128)(2,1)}), bf16[64,3,3584]{2,1,0:T(4,128)(2,1)S(1)}, u32[]{:S(2)}, u32[]{:S(2)}) async-start(bf16[64,3,3584]{2,1,0:T(4,128)(2,1)} %reshape.111), calls=%async_computation.2 | async-start | bytes 3670016 | tf_op jit(solution)/shard_map/all_to_all | solution.py:48
  78.1 56.4 %all-to-all-start = ((bf16[64,3,3584]{2,1,0:T(4,128)(2,1)}), bf16[64,3,3584]{2,1,0:T(4,128)(2,1)}, u32[]{:S(2)}, u32[]{:S(2)}) async-start(bf16[64,3,3584]{2,1,0:T(4,128)(2,1)} %reshape.107), calls=%async_computation | async-start | bytes 3670016 | tf_op jit(solution)/shard_map/all_to_all | solution.py:46
  85.7 134.5 %reduce-scatter.9.cloned.1.call-start = ((), (), s32[]{:S(2)}) async-start(), calls=%async_computation.7 | async-start | bytes 1949696
  88.2 2.2 copy-start.1
  88.2 2.2 copy-start.2
  88.2 2.2 copy-start.4
  93.8 252.8 %reduce-scatter.7.cloned.1.call-start = ((), (), s32[]{:S(2)}) async-start(), calls=%async_computation.6 | async-start | bytes 1949696
  144.8 87.0 %copy-start.6 = (f32[16,8]{0,1:T(8,128)S(1)}, f32[16,8]{0,1:T(8,128)}, u32[]{:S(2)}) copy-start(f32[16,8]{0,1:T(8,128)} %param.13) | copy-start | bytes 1540
  222.0 126.3 %all-to-all-start.3 = ((bf16[64,3,224]{2,1,0:T(4,128)(2,1)}), bf16[64,3,224]{2,1,0:T(4,128)(2,1)S(1)}, u32[]{:S(2)}, u32[]{:S(2)}) async-start(bf16[64,3,224]{2,1,0:T(4,128)(2,1)} %reshape.113), calls=%async_computation.3 | async-start | bytes 262144 | tf_op jit(solution)/shard_map/all_to_all | solution.py:83
  348.2 20.6 %all-to-all-start.1 = ((bf16[64,3,224]{2,1,0:T(4,128)(2,1)}), bf16[64,3,224]{2,1,0:T(4,128)(2,1)S(1)}, u32[]{:S(2)}, u32[]{:S(2)}) async-start(bf16[64,3,224]{2,1,0:T(4,128)(2,1)} %reshape.109), calls=%async_computation.1 | async-start | bytes 262144 | tf_op jit(solution)/shard_map/all_to_all | solution.py:82
Sparse Core Ops, SparseCore 0:
  93.9 126.3 reduce-scatter.8
  225.5 120.9 reduce-scatter.6
where the time goes:
time: 378 us; the launch traced here: 377 us
  waiting for transfers between devices  276 us (73%)
  starting transfers between devices  45.7 us (12%)
  local copies, waits for them, and re-layouts  28 us (7%)
  between operations  14.3 us (4%)
  matrix products  6.98 us (2%)
  other arithmetic  6.21 us (2%)
    unnamed x4, waiting for transfers between devices  190 us
    all_to_all x1, waiting for transfers between devices, body(): lax.all_to_all(send_a, 'expert', split_axis=0, concat_axis=0, tiled=True)  40.7 us
    all_to_all x1, waiting for transfers between devices, body(): lax.all_to_all(send_b, 'expert', split_axis=0, concat_axis=0, tiled=True)  36.2 us
    all_to_all x1, starting transfers between devices, body(): lax.all_to_all(send_b, 'expert', split_axis=0, concat_axis=0, tiled=True)  18.4 us
    all_to_all x1, starting transfers between devices, body(): lax.all_to_all(out_dx, 'expert', split_axis=0, concat_axis=0, tiled=True)  9.82 us
    all_to_all x1, starting transfers between devices, body(): lax.all_to_all(out_y, 'expert', split_axis=0, concat_axis=0, tiled=True)  9.76 us
    unnamed x22, local copies, waits for them, and re-layouts  9.67 us
    all_to_all x1, waiting for transfers between devices, body(): lax.all_to_all(out_y, 'expert', split_axis=0, concat_axis=0, tiled=True)  9.2 us
  transfers between devices with their start and end apart: 6, of which 5 were waited for; matrix products, arithmetic and copies ran while one was open for 8% of the time, Pallas kernels for 0%

commit v1 on v0

v1 whole, which is shorter than its diff:
```python
import functools

import jax
import jax.numpy as jnp
from jax import lax
from jax.experimental import pallas as pl
from jax.experimental.pallas import tpu as pltpu
from jax.sharding import PartitionSpec as P

NX, NZH, NY, NZL, NC = 4, 4, 8, 4, 2
TOK, TOP, RANKS = 16, 8, 3
D, FFL, SLOTS = 3584, 128, 192
Q = D // NX
COLS = D // (NX * NZH)
GRP = NZL * NC * 2
CH = RANKS * GRP
ROWS = NY * CH
LAG = 2
BF, F32, I32 = jnp.bfloat16, jnp.float32, jnp.int32
NEAR = (0, 1, 7, 2, 6, 3, 5, 4)
FAR = (4, 3, 5, 2, 6, 1, 7, 0)
HOPS = (
    [(dz, dc, kind) for dz in (1, -1) for dc in (0, 1) for kind in (2, 0, 1)]
    + [(2, dc, kind) for dc in (0, 1) for kind in (2, 0)]
    + [(-2, dc, 1) for dc in (0, 1)]
    + [(0, 1, kind) for kind in (2, 0, 1)]
)
NT = (((1,), (1,)), ((), ()))


def dot(a, b):
    return jnp.dot(a, b, preferred_element_type=F32)


def dot_nt(a, b):
    return lax.dot_general(a, b, NT, preferred_element_type=F32)


def iota(shape, axis):
    return lax.broadcasted_iota(I32, shape, axis)


def flag(cond):
    return jnp.where(cond, 1.0, 0.0)


def flatten_routes(table):
    shape = (TOK, TOK * TOP)
    row, lane = iota(shape, 0), iota(shape, 1)
    out = jnp.zeros(shape, F32)
    for k in range(TOP):
        hit = (lane >> 3 == row) & ((lane & 7) == k)
        out = out + jnp.where(hit, table[:, k : k + 1], 0.0)
    return jnp.sum(out, axis=0, keepdims=True)


def kernel(
    tok_a, tok_b, routes_a, routes_b, gates_a, gates_b, w_gate, w_up, w_down, sv_gate, sv_up,
    out_a, out_b,
    wg, wu, wd, sg, su,
    meta, met, tok, sel_t, send_y, rows, acc, hid, part, f1, f2, red, ret, dense, other, fin_src, fin,
    w_sem, own_sem, d1_s, d1_r, d2_s, d2_r, x_s, x_r, f_s, f_r,
    a_s, a_r, b_s, b_r, c_s, c_r, e_s, e_r, z_s, z_r,
):
    sec, exp = lax.axis_index("section"), lax.axis_index("expert")
    x, zh = lax.div(sec, NZH), lax.rem(sec, NZH)
    y, zl, c = lax.div(exp, NZL * NC), lax.rem(lax.div(exp, NC), NZL), lax.rem(exp, NC)
    z = zh * NZL + zl

    def at(dx=0, dy=0, dz=0, dc=0):
        z2 = lax.rem(z + (dz + 16), NZH * NZL)
        x2, y2, c2 = lax.rem(x + (dx + NX), NX), lax.rem(y + (dy + NY), NY), lax.rem(c + dc, NC)
        return (x2 * NZH + lax.div(z2, NZL), (y2 * NZL + lax.rem(z2, NZL)) * NC + c2)

    def remote(src, dst, s_sem, r_sem, where):
        return pltpu.make_async_remote_copy(
            src_ref=src, dst_ref=dst, send_sem=s_sem, recv_sem=r_sem,
            device_id=where, device_id_type=pl.DeviceIdType.MESH,
        )

    def ahead(dy):
        return lax.rem(y + dy, NY)

    loads = [pltpu.make_async_copy(sv_gate.at[0], sg, w_sem.at[0]),
             pltpu.make_async_copy(sv_up.at[0], su, w_sem.at[1])]
    for q in range(NX):
        span = pl.ds(q * Q, Q)
        loads.append(pltpu.make_async_copy(w_gate.at[0, span, :], wg.at[q], w_sem.at[2 + q]))
        loads.append(pltpu.make_async_copy(w_up.at[0, span, :], wu.at[q], w_sem.at[6 + q]))
        loads.append(pltpu.make_async_copy(w_down.at[0, :, span], wd.at[q], w_sem.at[10 + q]))
    for load in loads:
        load.start()

    barrier = pltpu.get_barrier_semaphore()
    peers = [at(dx=1), at(dx=-1)] + [at(dy=d) for d in range(1, NY)]
    peers += [at(dz=d) for d in range(1, 16)]
    peers += [at(dz=d, dc=1) for d in (-2, -1, 0, 1, 2)]
    for peer in peers:
        pl.semaphore_signal(barrier, inc=1, device_id=peer, device_id_type=pl.DeviceIdType.MESH)

    meta[...] = jnp.zeros((8, TOK * TOP), F32)
    meta[0:1, :] = flatten_routes(routes_a[...].astype(F32))
    meta[1:2, :] = flatten_routes(routes_b[...].astype(F32))
    meta[2:3, :] = flatten_routes(gates_a[...])
    meta[3:4, :] = flatten_routes(gates_b[...])
    pl.semaphore_wait(barrier, len(peers))

    block = c * NZL + zl
    columns = pl.ds(pl.multiple_of(x * Q, 128), Q)

    def landing(blk, kind):
        if kind == 2:
            return met.at[blk]
        return tok.at[pl.ds(pl.multiple_of((blk * 2 + kind) * TOK, TOK), TOK), :]

    def source(kind):
        return meta if kind == 2 else (tok_a, tok_b)[kind].at[:, columns]

    gather = [
        remote(source(kind), landing(block, kind), d1_s.at[n], d1_r.at[n], at(dz=dz, dc=dc))
        for n, (dz, dc, kind) in enumerate(HOPS)
    ]
    for copy in gather:
        copy.start()
    own = [pltpu.make_async_copy(source(kind), landing(block, kind), own_sem.at[kind]) for kind in range(3)]
    for copy in own:
        copy.start()
    for copy in own:
        copy.wait()
    for copy in gather:
        copy.wait_recv()

    sq = (128, 128)
    row, lane = iota(sq, 0), iota(sq, 1)
    small = iota((GRP, 128), 0)
    route_g, gate_g = jnp.zeros((GRP, 128), F32), jnp.zeros((GRP, 128), F32)
    for g in range(GRP):
        route_g = jnp.where(small == g, met[g // 2, g % 2 : g % 2 + 1, :], route_g)
        gate_g = jnp.where(small == g, met[g // 2, 2 + g % 2 : 3 + g % 2, :], gate_g)
    route_t = jnp.concatenate([route_g] * NY, axis=0)
    gate_t = jnp.concatenate([gate_g] * NY, axis=0)
    expert_id = (((row >> 4) * NZL + zl) * NC + c).astype(F32)
    named = flag(route_t == expert_id)
    before = dot(named.astype(BF), flag(row < lane).astype(BF))
    wide, tall = (128, 256), (256, 128)
    spread = flag((iota(wide, 0) >> 3) == (iota(wide, 1) & 15)).astype(BF)
    spread_t = flag((iota(tall, 1) >> 3) == (iota(tall, 0) & 15)).astype(BF)
    same = (iota(wide, 0) & 15) == (iota(wide, 1) >> 4)
    same_t = (iota(tall, 1) & 15) == (iota(tall, 0) >> 4)
    of_b = (row & 1) == 1
    for r in range(RANKS):
        hit = jnp.where(before == float(r), named, 0.0)
        pick = jnp.where(same, dot(hit.astype(BF), spread), 0.0).astype(BF)
        weight = hit * gate_t
        gate_row = jnp.sum(weight, axis=1, keepdims=True)
        scale = jnp.where((iota((128, 1), 0) & 1) == 1, gate_row, 1.0)
        picked = (dot(pick, tok[...]) * scale).astype(BF)
        send_y[:, r * GRP : (r + 1) * GRP, :] = picked.reshape(NY, GRP, Q)
        weight = jnp.where(of_b, hit, weight)
        high = weight.astype(BF)
        low = (weight - high.astype(F32)).astype(BF)
        sel_t[0, r] = jnp.where(same_t, dot_nt(spread_t, high), 0.0).astype(BF)
        sel_t[1, r] = jnp.where(same_t, dot_nt(spread_t, low), 0.0).astype(BF)

    def y_copy(dy):
        return remote(send_y.at[ahead(dy)], rows.at[x, y], d2_s.at[dy], d2_r.at[NY - dy], at(dy=dy))

    def y_wait(dy):
        remote(send_y.at[ahead(dy)], rows.at[x, ahead(dy)], d2_s.at[dy], d2_r.at[dy], at(dy=dy)).wait_recv()

    mine = pltpu.make_async_copy(send_y.at[y], rows.at[x, y], own_sem.at[0])
    mine.start()
    y_copies = [y_copy(dy) for dy in NEAR[1:]]
    for copy in y_copies:
        copy.start()

    left, right = lax.rem(x + NX - 1, NX), lax.rem(x + 1, NX)
    opposite = lax.rem(x + 2, NX)
    x_copies, forwards = [], []

    def x_copy(side, i, quarter, yc):
        ref = rows.at[quarter, yc]
        return remote(ref, ref, x_s.at[side, i], x_r.at[side, i], at(dx=1 - 2 * side))

    def forward(i, quarter, yc):
        ref = rows.at[quarter, yc]
        return remote(ref, ref, f_s.at[i], f_r.at[i], at(dx=1 if i % 2 == 0 else -1))

    for i in range(NY + LAG):
        if i < NY:
            if i == 0:
                mine.wait()
            else:
                y_wait(NEAR[i])
            for side in range(2):
                copy = x_copy(side, i, x, ahead(NEAR[i]))
                copy.start()
                x_copies.append(copy)
        j = i - LAG
        if j >= 0:
            yj = ahead(NEAR[j])
            x_copy(0, j, left, yj).wait_recv()
            x_copy(1, j, right, yj).wait_recv()
            copy = forward(j, left if j % 2 == 0 else right, yj)
            copy.start()
            forwards.append(copy)

    for load in loads:
        load.wait()

    def project(step, quarter):
        block_rows = rows[quarter].reshape(ROWS, Q)
        for n, value in enumerate((dot(block_rows, wg[quarter]), dot(block_rows, wu[quarter]),
                                   dot_nt(block_rows, wd[quarter]))):
            if step:
                value = acc[n] + value
            acc[n] = value

    for step, quarter in enumerate((x, left, right)):
        project(step, quarter)

    tallrow = iota((ROWS, SLOTS), 0)
    chunk_of = (tallrow * 1366) >> 16
    inner = tallrow - chunk_of * CH
    slot = (chunk_of * (NZL * NC) + ((inner >> 1) & 3) * NC + ((inner >> 3) & 1)) * RANKS + (inner >> 4)
    place = flag(slot == iota((ROWS, SLOTS), 1)).astype(BF)
    pre_gate, pre_up = dot(place, sg[...]), dot(place, su[...])
    squash = 1.0 / (1.0 + jnp.exp(-pre_gate))

    for i in range(NY):
        forward(i, opposite, ahead(NEAR[i])).wait_recv()
    project(3, opposite)

    is_b = (iota((ROWS, FFL), 0) & 1) == 1
    gate_pre, up_pre, grad = acc[0], acc[1], acc[2]
    value = gate_pre / (1.0 + jnp.exp(-gate_pre)) * up_pre
    hid[0] = jnp.where(is_b, 0.0, value).astype(BF)
    grad_up = grad * (pre_gate * squash)
    grad_gate = grad * pre_up * squash * (1.0 + pre_gate * (1.0 - squash))
    hid[1] = jnp.where(is_b, grad_gate, 0.0).astype(BF)
    hid[2] = jnp.where(is_b, grad_up, 0.0).astype(BF)

    def expand(n, quarter):
        value = dot(hid[0], wd[quarter]) + dot_nt(hid[1], wg[quarter]) + dot_nt(hid[2], wu[quarter])
        part[n] = value.astype(BF).reshape(NY, CH, Q)

    sends = []

    def go(copy):
        copy.start()
        sends.append(copy)

    def first_copy(i, yc):
        return remote(part.at[2, yc], f1.at[yc], a_s.at[i], a_r.at[i], at(dx=1 if i % 2 == 0 else -1))

    def second_copy(side, i, yc):
        return remote(part.at[side, yc], f2.at[side, yc], b_s.at[side, i], b_r.at[side, i], at(dx=1 - 2 * side))

    expand(2, opposite)
    for i in range(NY):
        go(first_copy(i, ahead(FAR[i])))
    for side, quarter in enumerate((right, left)):
        expand(side, quarter)
        for i in range(NY):
            if i % 2 != side:
                go(second_copy(side, i, ahead(FAR[i])))
    for i in range(NY):
        yc, side = ahead(FAR[i]), i % 2
        first_copy(i, yc).wait_recv()
        part[side, yc] = (part[side, yc].astype(F32) + f1[yc].astype(F32)).astype(BF)
        go(second_copy(side, i, yc))
    expand(3, x)

    def back_copy(dy):
        return remote(red.at[ahead(dy)], ret.at[y], c_s.at[dy], c_r.at[NY - dy], at(dy=dy))

    for i in range(NY):
        yc, dy = ahead(FAR[i]), FAR[i]
        second_copy(0, i, yc).wait_recv()
        second_copy(1, i, yc).wait_recv()
        total = part[3, yc].astype(F32) + f2[0, yc].astype(F32) + f2[1, yc].astype(F32)
        if dy:
            red[yc] = total.astype(BF)
            go(back_copy(dy))
        else:
            ret[yc] = total.astype(BF)
    for dy in FAR[:-1]:
        remote(red.at[ahead(dy)], ret.at[ahead(dy)], c_s.at[dy], c_r.at[dy], at(dy=dy)).wait_recv()

    total = jnp.zeros((256, Q), F32)
    for r in range(RANKS):
        back = ret[:, r * GRP : (r + 1) * GRP, :].reshape(NY * GRP, Q)
        total = total + dot(sel_t[0, r], back) + dot(sel_t[1, r], back)
    dense[...] = total.astype(BF).reshape(NC, 128, Q)
    core_copy = remote(dense.at[1 - c], other, e_s.at[0], e_r.at[0], at(dc=1))
    core_copy.start()
    core_copy.wait_recv()
    both = dense[c].astype(F32) + other[...].astype(F32)
    for h in range(NZH):
        turned = both if h == 0 else pltpu.roll(both, Q - h * COLS, axis=1)
        fin_src[h] = turned[:, 0:256].astype(BF).reshape(NZL, 2 * TOK, 256)

    def z_copy(dz):
        z2 = lax.rem(z + dz, 16)
        return remote(fin_src.at[lax.div(z2, NZL), lax.rem(z2, NZL)], fin.at[dz], z_s.at[dz], z_r.at[dz], at(dz=dz))

    z_order = sorted(range(1, 16), key=lambda d: -min(d, 16 - d))
    z_copies = [z_copy(dz) for dz in z_order]
    for copy in z_copies:
        copy.start()
    result = fin_src[zh, zl].astype(F32)
    for dz in reversed(z_order):
        z_copy(dz).wait_recv()
        result = result + fin[dz].astype(F32)
    out_a[...] = result[0:TOK, 0:COLS].astype(BF)
    out_b[...] = result[TOK : 2 * TOK, 0:COLS].astype(BF)

    for copy in gather + y_copies + x_copies + forwards + sends + [core_copy] + z_copies:
        copy.wait_send()


def body(tokens_a, routes_a, gates_a, cotangent_b, routes_b, gates_b,
         gate_weight, up_weight, down_weight, saved_gate, saved_up):
    far, near = pl.BlockSpec(memory_space=pl.ANY), pl.BlockSpec(memory_space=pltpu.VMEM)
    dma = lambda *shape: pltpu.SemaphoreType.DMA(shape)
    vmem = lambda dtype, *shape: pltpu.VMEM(shape, dtype)
    out = jax.ShapeDtypeStruct((TOK, COLS), BF)
    hops = len(HOPS)
    return pl.pallas_call(
        kernel,
        out_shape=(out, out),
        in_specs=[far, far, near, near, near, near, far, far, far, far, far],
        out_specs=(near, near),
        scratch_shapes=[
            vmem(BF, NX, Q, FFL), vmem(BF, NX, Q, FFL), vmem(BF, NX, FFL, Q),
            vmem(BF, SLOTS, FFL), vmem(BF, SLOTS, FFL),
            vmem(F32, 8, 128), vmem(F32, NZL * NC, 8, 128), vmem(BF, 256, Q),
            vmem(BF, 2, RANKS, 256, 128), vmem(BF, NY, CH, Q), vmem(BF, NX, NY, CH, Q),
            vmem(F32, 3, ROWS, FFL), vmem(BF, 3, ROWS, FFL), vmem(BF, NX, NY, CH, Q),
            vmem(BF, NY, CH, Q), vmem(BF, 2, NY, CH, Q), vmem(BF, NY, CH, Q), vmem(BF, NY, CH, Q),
            vmem(BF, NC, 128, Q), vmem(BF, 128, Q),
            vmem(BF, NZH, NZL, 2 * TOK, 256), vmem(BF, 16, 2 * TOK, 256),
            dma(14), dma(3), dma(hops), dma(hops), dma(NY), dma(NY), dma(2, NY), dma(2, NY), dma(NY), dma(NY),
            dma(NY), dma(NY), dma(2, NY), dma(2, NY), dma(NY), dma(NY), dma(1), dma(1), dma(16), dma(16),
        ],
        compiler_params=pltpu.CompilerParams(
            collective_id=0, has_side_effects=True, vmem_limit_bytes=60 * 1024 * 1024
        ),
        name="routed_experts",
    )(tokens_a, cotangent_b, routes_a, routes_b, gates_a, gates_b,
      gate_weight, up_weight, down_weight, saved_gate, saved_up)


def solution(mesh):
    placed = (
        P("expert", None), P("expert", None), P("expert", None),
        P("expert", None), P("expert", None), P("expert", None),
        P("expert", None, "section"), P("expert", None, "section"), P("expert", "section", None),
        P("expert", None, "section"), P("expert", None, "section"),
    )
    return jax.shard_map(
        body, mesh=mesh, in_specs=placed,
        out_specs=(P("expert", "section"), P("expert", "section")), check_vma=False,
    )
```

time: 378 us -> 119 us (0.31)
  waiting for transfers between devices: 276 us -> 0 us
  Pallas kernels: 0 us -> 112 us
  starting transfers between devices: 45.7 us -> 0 us
  local copies, waits for them, and re-layouts: 28 us -> 5.3 us
  between operations: 14.3 us -> 0.66 us
  matrix products: 6.98 us -> 0 us
  other arithmetic: 6.21 us -> 0 us
    unnamed x4 -> x0, waiting for transfers between devices: 190 us -> none
    pallas_call x0 -> x1, Pallas kernels: none -> 112 us  [body(): pl.pallas_call(kernel, out_shape=(out, out), in_specs=[far, far, near, ne...]
    all_to_all x4 -> x0, waiting for transfers between devices: 86.1 us -> none  [the longest x1 40.7 us: body(): lax.all_to_all(send_a, 'expert', split_axis=0, concat_axis=0, tiled=True)]
    all_to_all x4 -> x0, starting transfers between devices: 45.6 us -> none  [the longest x1 18.4 us: body(): lax.all_to_all(send_b, 'expert', split_axis=0, concat_axis=0, tiled=True)]
    reshape x8 -> x0, local copies, waits for them, and re-layouts: 13 us -> none  [the longest x1 3.92 us: body(): fill_slots(values_a, where_a, slot_count)]
    dot_general x5 -> x0, matrix products: 6.98 us -> none  [the longest x1 3.23 us: body(): part_y = jnp.dot(hidden, w_down, preferred_element_type=jnp.float32)]
    unnamed x22 -> x14, local copies, waits for them, and re-layouts: 9.67 us -> 5.3 us
  transfers between devices with their start and end apart: 6 -> 0, of which waited for: 5 -> 0; matrix products, arithmetic and copies ran while one was open for 8% -> 0% of each run, Pallas kernels for 0% -> 0%
where the time goes in v1:
time: 119 us; the launch traced here: 118 us
  Pallas kernels  112 us (94%)
  local copies, waits for them, and re-layouts  5.3 us (4%)
    pallas_call x1, Pallas kernels, body(): pl.pallas_call(kernel, out_shape=(out, out), in_specs=[far, far, near, ne...  112 us
    unnamed x14, local copies, waits for them, and re-layouts  5.3 us

profile of v1, /device:TPU:1, one launch (start us, length us, event | category | flops | bytes accessed | tf_op | source)
XLA Modules:
  0.0 118.2 jit_solution(14224621651083690485)
XLA Ops:
  0.6 0.0 copy-start.1
  0.6 1.4 %copy.13.routes_a = s32[16,8]{1,0:T(8,128)} copy(s32[16,8]{0,1:T(8,128)} %param.12) | data formatting | bytes 1024 | tf_op args[1]
  2.0 0.0 copy-done.1
  2.0 0.0 copy-start.2
  2.0 0.7 copy.15.gates_a
  2.7 0.0 copy-done.2
  2.7 0.0 copy-start.3
  2.7 0.7 copy.14.routes_b
  3.4 0.0 copy-done.3
  3.4 0.7 copy.16.gates_b
  4.0 112.2 %routed_experts.1 = (bf16[16,224]{1,0:T(8,128)(2,1)}, bf16[16,224]{1,0:T(8,128)(2,1)}) custom-call(bf16[16,3584]{1,0:T(8,128)(2,1)} %tok_a.1, bf16[16,3584]{1,0:T(8,128)(2,1)} %tok_b.1, s32[16,8]{1,0:T(8,128)} %copy.13.routes_a, s32[16,8]{1,0:T(8,128)} %copy.14.routes_b, f32[16,8]{1,0:T(8,128)} %copy.15.gates_a, f32[16,8]{1,0:T(8,128)} %copy.16.gates_b, ...), custom_call_target="tpu_custom_call" | custom-call | tf_op jit(solution)/shard_map/routed_experts/pallas_call | solution.py:329
  116.3 0.0 copy-start
  116.3 1.3 %copy.19 = bf16[16,224]{1,0:T(8,128)(2,1)} copy(bf16[16,224]{1,0:T(8,128)(2,1)} %get-tuple-element.4) | data formatting | bytes 14336
  117.6 0.0 copy-done
  117.6 0.6 copy.20
Async XLA Ops:
  0.6 1.4 %copy-start.1 = (f32[16,8]{0,1:T(8,128)S(1)}, f32[16,8]{0,1:T(8,128)}, u32[]{:S(2)}) copy-start(f32[16,8]{0,1:T(8,128)} %param.13) | copy-start | bytes 1540
  2.0 0.7 copy-start.2
  2.7 0.7 copy-start.3
  116.3 1.3 %copy-start = (bf16[16,224]{1,0:T(8,128)(2,1)S(1)}, bf16[16,224]{1,0:T(8,128)(2,1)}, u32[]{:S(2)}) copy-start(bf16[16,224]{1,0:T(8,128)(2,1)} %get-tuple-element.5) | copy-start | bytes 21508

commit v2 on v1

v2 whole, which is shorter than its diff:
```python
import functools

import jax
import jax.numpy as jnp
from jax import lax
from jax.experimental import pallas as pl
from jax.experimental.pallas import tpu as pltpu
from jax.sharding import PartitionSpec as P

NX, NZH, NY, NZL, NC = 4, 4, 8, 4, 2
TOK, TOP, RANKS = 16, 8, 3
D, FFL, SLOTS = 3584, 128, 192
Q = D // NX
COLS = D // (NX * NZH)
GRP = NZL * NC * 2
CH = RANKS * GRP
ROWS = NY * CH
HALF = NY // 2
BF, F32, I32 = jnp.bfloat16, jnp.float32, jnp.int32
NEAR = (0, 1, 7, 2, 6, 3, 5, 4)
POS = (0, 1, 3, 5, 7, 6, 4, 2)
CUTS = ((0, 512), (512, 384))
TURNS = ((0, 256, 0), (128, 384, 96), (384, 384, 64), (640, 256, 32))
HOPS = (
    [(dz, dc, kind) for dz in (1, -1) for dc in (0, 1) for kind in (2, 0, 1)]
    + [(2, dc, kind) for dc in (0, 1) for kind in (2, 0)]
    + [(-2, dc, 1) for dc in (0, 1)]
    + [(0, 1, kind) for kind in (2, 0, 1)]
)
NT = (((1,), (1,)), ((), ()))


def dot(a, b):
    return jnp.dot(a, b, preferred_element_type=F32)


def dot_nt(a, b):
    return lax.dot_general(a, b, NT, preferred_element_type=F32)


def iota(shape, axis):
    return lax.broadcasted_iota(I32, shape, axis)


def flag(cond):
    return jnp.where(cond, 1.0, 0.0)


def flatten_routes(table):
    shape = (TOP, TOK * TOP)
    row, lane = iota(shape, 0), iota(shape, 1)
    out = jnp.zeros(shape, F32)
    for t in range(TOK):
        hit = (lane >> 4 == row) & ((lane & 15) == t)
        out = out + jnp.where(hit, table[:, t : t + 1], 0.0)
    return jnp.sum(out, axis=0, keepdims=True)


def kernel(
    tok_a, tok_b, routes_a, routes_b, gates_a, gates_b, w_gate, w_up, w_down, sv_gate, sv_up,
    out,
    wg, wu, wd, sg, su,
    meta, met, tok, sel_t, send_y, rows, acc, hid, part, f1, f2, red, ret, dense, other, tot, fin_src, fin,
    w_sem, own_sem, d1_s, d1_r, d2_s, d2_r, x_s, x_r, f_s, f_r,
    a_s, a_r, b_s, b_r, c_s, c_r, e_s, e_r, z_s, z_r,
):
    sec, exp = lax.axis_index("section"), lax.axis_index("expert")
    x, zh = lax.div(sec, NZH), lax.rem(sec, NZH)
    y, zl, c = lax.div(exp, NZL * NC), lax.rem(lax.div(exp, NC), NZL), lax.rem(exp, NC)
    z = zh * NZL + zl

    def at(dx=0, dy=0, dz=0, dc=0):
        z2 = lax.rem(z + (dz + 16), NZH * NZL)
        x2, y2, c2 = lax.rem(x + (dx + NX), NX), lax.rem(y + (dy + NY), NY), lax.rem(c + dc, NC)
        return (x2 * NZH + lax.div(z2, NZL), (y2 * NZL + lax.rem(z2, NZL)) * NC + c2)

    def remote(src, dst, s_sem, r_sem, where):
        return pltpu.make_async_remote_copy(
            src_ref=src, dst_ref=dst, send_sem=s_sem, recv_sem=r_sem,
            device_id=where, device_id_type=pl.DeviceIdType.MESH,
        )

    barrier = pltpu.get_barrier_semaphore()
    peers = [at(dx=1), at(dx=-1)] + [at(dy=d) for d in range(1, NY)]
    peers += [at(dz=d) for d in range(1, 16)]
    peers += [at(dz=d, dc=1) for d in (-2, -1, 0, 1, 2)]
    for peer in peers:
        pl.semaphore_signal(barrier, inc=1, device_id=peer, device_id_type=pl.DeviceIdType.MESH)

    loads = [pltpu.make_async_copy(sv_gate.at[0], sg, w_sem.at[0]),
             pltpu.make_async_copy(sv_up.at[0], su, w_sem.at[1])]
    for q in range(NX):
        span = pl.ds(q * Q, Q)
        loads.append(pltpu.make_async_copy(w_gate.at[0, span, :], wg.at[q], w_sem.at[2 + q]))
        loads.append(pltpu.make_async_copy(w_up.at[0, span, :], wu.at[q], w_sem.at[6 + q]))
        loads.append(pltpu.make_async_copy(w_down.at[0, :, span], wd.at[q], w_sem.at[10 + q]))
    for load in loads:
        load.start()

    meta[...] = jnp.zeros((8, TOK * TOP), F32)
    meta[0:1, :] = flatten_routes(routes_a[...].astype(F32))
    meta[1:2, :] = flatten_routes(routes_b[...].astype(F32))
    meta[2:3, :] = flatten_routes(gates_a[...])
    meta[3:4, :] = flatten_routes(gates_b[...])
    pl.semaphore_wait(barrier, len(peers))

    block = c * NZL + zl
    columns = pl.ds(pl.multiple_of(x * Q, 128), Q)

    def landing(blk, kind):
        if kind == 2:
            return met.at[blk]
        return tok.at[pl.ds(pl.multiple_of((blk * 2 + kind) * TOK, TOK), TOK), :]

    def source(kind):
        return meta if kind == 2 else (tok_a, tok_b)[kind].at[:, columns]

    gather = [
        remote(source(kind), landing(block, kind), d1_s.at[n], d1_r.at[n], at(dz=dz, dc=dc))
        for n, (dz, dc, kind) in enumerate(HOPS)
    ]
    own = [pltpu.make_async_copy(source(kind), landing(block, kind), own_sem.at[kind]) for kind in range(3)]
    for meta_first in (True, False):
        for n, (_, _, kind) in enumerate(HOPS):
            if (kind == 2) == meta_first:
                gather[n].start()
    for copy in own:
        copy.start()
    for copy in own:
        copy.wait()
    for n, (_, _, kind) in enumerate(HOPS):
        if kind == 2:
            gather[n].wait_recv()

    sq = (128, 128)
    row, lane = iota(sq, 0), iota(sq, 1)
    small = iota((GRP, 128), 0)
    route_g, gate_g = jnp.zeros((GRP, 128), F32), jnp.zeros((GRP, 128), F32)
    for g in range(GRP):
        route_g = jnp.where(small == g, met[g // 2, g % 2 : g % 2 + 1, :], route_g)
        gate_g = jnp.where(small == g, met[g // 2, 2 + g % 2 : 3 + g % 2, :], gate_g)
    route_t = jnp.concatenate([route_g] * NY, axis=0)
    gate_t = jnp.concatenate([gate_g] * NY, axis=0)
    expert_id = (((((row >> 4) + y) & 7) * NZL + zl) * NC + c).astype(F32)
    named = flag(route_t == expert_id)
    before = dot(named.astype(BF), flag((row & 15) < (lane & 15)).astype(BF))
    wide, tall = (128, 256), (256, 128)
    spread = flag((iota(wide, 0) & 15) == (iota(wide, 1) & 15)).astype(BF)
    same = (iota(wide, 0) & 15) == (iota(wide, 1) >> 4)
    picks = []
    for r in range(RANKS):
        hit = jnp.where(before == float(r), named, 0.0)
        pick = jnp.where(same, dot(hit.astype(BF), spread), 0.0).astype(BF)
        gate_row = jnp.sum(hit * gate_t, axis=1, keepdims=True)
        picks.append((pick, jnp.where((iota((128, 1), 0) & 1) == 1, gate_row, 1.0)))

    for n, (_, _, kind) in enumerate(HOPS):
        if kind != 2:
            gather[n].wait_recv()
    for r in range(RANKS):
        pick, scale = picks[r]
        picked = (dot(pick, tok[...]) * scale).astype(BF)
        slab = slice(r * GRP, (r + 1) * GRP)
        rows[0, 0, slab, :] = picked[0:GRP]
        send_y[:, slab, :] = picked[GRP:].reshape(NY - 1, GRP, Q)

    def y_copy(d):
        return remote(send_y.at[d - 1], rows.at[0, POS[NY - d]], d2_s.at[d], d2_r.at[NY - d], at(dy=d))

    x_copies, forwards = [], []

    def x_copy(side, p):
        return remote(rows.at[0, p], rows.at[3 - 2 * side, p], x_s.at[side, p], x_r.at[side, p], at(dx=1 - 2 * side))

    def forward(p):
        return remote(rows.at[3 if p % 2 == 0 else 1, p], rows.at[2, p], f_s.at[p], f_r.at[p],
                      at(dx=1 if p % 2 == 0 else -1))

    def x_step(p):
        if p:
            y_copy(NY - NEAR[p]).wait_recv()
        for side in range(2):
            x_copies.append(x_copy(side, p))
            x_copies[-1].start()

    def x_forward(p):
        x_copy(0, p).wait_recv()
        x_copy(1, p).wait_recv()
        forwards.append(forward(p))
        forwards[-1].start()

    y_copies = [y_copy(d) for d in NEAR[1:]]
    for copy in y_copies:
        copy.start()
    x_step(0)

    spread_t = flag((iota(tall, 1) & 15) == (iota(tall, 0) & 15)).astype(BF)
    same_t = (iota(tall, 1) & 15) == (iota(tall, 0) >> 4)
    of_b = (row & 1) == 1
    for r in range(RANKS):
        hit = jnp.where(before == float(r), named, 0.0)
        weight = jnp.where(of_b, hit, hit * gate_t)
        high = weight.astype(BF)
        low = (weight - high.astype(F32)).astype(BF)
        sel_t[0, r] = jnp.where(same_t, dot_nt(spread_t, high), 0.0).astype(BF)
        sel_t[1, r] = jnp.where(same_t, dot_nt(spread_t, low), 0.0).astype(BF)
    for load in loads:
        load.wait()

    mine = HALF * CH
    is_b = (iota((mine, FFL), 0) & 1) == 1

    def quarter(k):
        return lax.rem(x + k, NX)

    def project(h, k):
        block_rows = rows[k, h * HALF : (h + 1) * HALF].reshape(mine, Q)
        q = quarter(k)
        for n, value in enumerate((dot(block_rows, wg[q]), dot(block_rows, wu[q]), dot_nt(block_rows, wd[q]))):
            acc[n] = value if k == 0 else acc[n] + value

    def activate(h):
        at_row = iota((mine, SLOTS), 0)
        chunk = (at_row * 1366) >> 16
        inner = at_row - chunk * CH
        shift = jnp.full((mine, SLOTS), NEAR[h * HALF], I32)
        for i in range(1, HALF):
            shift = jnp.where(chunk == i, NEAR[h * HALF + i], shift)
        blk = ((shift + y) & 7) * (NZL * NC) + ((inner >> 1) & 3) * NC + ((inner >> 3) & 1)
        place = flag(blk * RANKS + (inner >> 4) == iota((mine, SLOTS), 1)).astype(BF)
        pre_gate, pre_up = dot(place, sg[...]), dot(place, su[...])
        squash = 1.0 / (1.0 + jnp.exp(-pre_gate))
        gate_pre, up_pre, grad = acc[0], acc[1], acc[2]
        value = gate_pre / (1.0 + jnp.exp(-gate_pre)) * up_pre
        hid[0] = jnp.where(is_b, 0.0, value).astype(BF)
        grad_up = grad * (pre_gate * squash)
        grad_gate = grad * pre_up * squash * (1.0 + pre_gate * (1.0 - squash))
        hid[1] = jnp.where(is_b, grad_gate, 0.0).astype(BF)
        hid[2] = jnp.where(is_b, grad_up, 0.0).astype(BF)

    def expand(h, k):
        q = quarter(k)
        value = dot(hid[0], wd[q]) + dot_nt(hid[1], wg[q]) + dot_nt(hid[2], wu[q])
        part[k, h * HALF : (h + 1) * HALF] = value.astype(BF).reshape(HALF, CH, Q)

    sends = []

    def go(copy):
        copy.start()
        sends.append(copy)

    def cols(s):
        return slice(CUTS[s][0], CUTS[s][0] + CUTS[s][1])

    def half(h):
        return range(h * HALF, (h + 1) * HALF)

    def first_copy(s, p):
        return remote(part.at[2, p, :, cols(s)], f1.at[p, :, cols(s)], a_s.at[s, p], a_r.at[s, p],
                      at(dx=1 if p % 2 == 0 else -1))

    def second_copy(s, side, p):
        return remote(part.at[1 + 2 * side, p, :, cols(s)], f2.at[side, p, :, cols(s)],
                      b_s.at[s, side, p], b_r.at[s, side, p], at(dx=1 - 2 * side))

    def send_first(s, h):
        for p in half(h):
            go(first_copy(s, p))

    def send_plain(s, h):
        for p in half(h):
            go(second_copy(s, 1 - p % 2, p))

    def send_added(s, h):
        for p in half(h):
            first_copy(s, p).wait_recv()
            k = 1 + 2 * (p % 2)
            total = part[k, p, :, cols(s)].astype(F32) + f1[p, :, cols(s)].astype(F32)
            part[k, p, :, cols(s)] = total.astype(BF)
            go(second_copy(s, p % 2, p))

    def back_copy(s, d):
        return remote(red.at[d, :, cols(s)], ret.at[(NY - d) % NY, :, cols(s)],
                      c_s.at[s, d], c_r.at[s, (NY - d) % NY], at(dy=d))

    def finish(s):
        for p in reversed(range(NY)):
            second_copy(s, 0, p).wait_recv()
            second_copy(s, 1, p).wait_recv()
            total = part[0, p, :, cols(s)].astype(F32) + f2[0, p, :, cols(s)].astype(F32)
            total = (total + f2[1, p, :, cols(s)].astype(F32)).astype(BF)
            d = NEAR[p]
            if d:
                red[d, :, cols(s)] = total
                go(back_copy(s, d))
            else:
                ret[0, :, cols(s)] = total

    def core_copy(s):
        return remote(dense.at[1 - c, :, cols(s)], other.at[:, cols(s)], e_s.at[s], e_r.at[s], at(dc=1))

    def combine(s):
        for d in range(1, NY):
            back_copy(s, NY - d).wait_recv()
        width = CUTS[s][1]
        total = jnp.zeros((256, width), F32)
        for r in range(RANKS):
            back = ret[:, r * GRP : (r + 1) * GRP, cols(s)].reshape(NY * GRP, width)
            total = total + dot(sel_t[0, r], back) + dot(sel_t[1, r], back)
        dense[:, :, cols(s)] = total.astype(BF).reshape(NC, 128, width)
        go(core_copy(s))

    def z_copy(zh2, zl2):
        behind = lax.rem(z + (16 - (zh2 * NZL + zl2)), 16)
        return remote(fin_src.at[zh2, zl2], fin.at[behind], z_s.at[zh2, zl2], z_r.at[behind],
                      (x * NZH + zh2, (y * NZL + zl2) * NC + c))

    def scatter(s):
        core_copy(s).wait_recv()
        tot[:, cols(s)] = dense[c, :, cols(s)].astype(F32) + other[:, cols(s)].astype(F32)
        for h in (2 * s, 2 * s + 1):
            base, width, shift = TURNS[h]
            turned = tot[:, base : base + width]
            if shift:
                turned = pltpu.roll(turned, width - shift, axis=1)
            fin_src[h] = turned[:, 0:256].astype(BF).reshape(NZL, 2 * TOK, 256)
        for h in (2 * s, 2 * s + 1):
            for l in range(NZL):
                @pl.when(z != h * NZL + l)
                def _():
                    z_copy(h, l).start()

    for p in range(HALF + 1):
        if p:
            x_step(p)
            x_forward(p - 1)
    for k in (0, 3, 1):
        project(0, k)
    for p in (5, 6):
        x_step(p)
        x_forward(p - 1)
    for p in half(0):
        forward(p).wait_recv()
    project(0, 2)
    activate(0)
    expand(0, 2)
    send_first(0, 0)
    for k in (1, 3):
        expand(0, k)
    send_plain(0, 0)
    x_step(7)
    x_forward(6)
    project(1, 0)
    send_added(0, 0)
    expand(0, 0)
    x_forward(7)
    for k in (3, 1):
        project(1, k)
    for p in half(1):
        forward(p).wait_recv()
    project(1, 2)
    activate(1)
    expand(1, 2)
    send_first(0, 1)
    for k in (1, 3):
        expand(1, k)
    send_plain(0, 1)
    send_first(1, 0)
    send_added(0, 1)
    send_first(1, 1)
    for h in range(2):
        send_plain(1, h)
    expand(1, 0)
    for h in range(2):
        send_added(1, h)
    finish(0)
    combine(0)
    scatter(0)
    finish(1)
    combine(1)
    scatter(1)

    result = fin_src[zh, zl].astype(F32)
    for behind in sorted(range(1, 16), key=lambda d: min(d, 16 - d)):
        remote(fin_src.at[0, 0], fin.at[behind], z_s.at[0, 0], z_r.at[behind], at(dz=1)).wait_recv()
        result = result + fin[behind].astype(F32)
    out[...] = result[:, 0:COLS].astype(BF)

    for copy in gather + y_copies + x_copies + forwards + sends:
        copy.wait_send()
    for h in range(NZH):
        for l in range(NZL):
            @pl.when(z != h * NZL + l)
            def _():
                z_copy(h, l).wait_send()


def body(tokens_a, routes_a, gates_a, cotangent_b, routes_b, gates_b,
         gate_weight, up_weight, down_weight, saved_gate, saved_up):
    far, near = pl.BlockSpec(memory_space=pl.ANY), pl.BlockSpec(memory_space=pltpu.VMEM)
    dma = lambda *shape: pltpu.SemaphoreType.DMA(shape)
    vmem = lambda dtype, *shape: pltpu.VMEM(shape, dtype)
    hops, mine = len(HOPS), HALF * CH
    both = pl.pallas_call(
        kernel,
        out_shape=jax.ShapeDtypeStruct((2 * TOK, COLS), BF),
        in_specs=[far, far, near, near, near, near, far, far, far, far, far],
        out_specs=near,
        scratch_shapes=[
            vmem(BF, NX, Q, FFL), vmem(BF, NX, Q, FFL), vmem(BF, NX, FFL, Q),
            vmem(BF, SLOTS, FFL), vmem(BF, SLOTS, FFL),
            vmem(F32, 8, 128), vmem(F32, NZL * NC, 8, 128), vmem(BF, 256, Q),
            vmem(BF, 2, RANKS, 256, 128), vmem(BF, NY - 1, CH, Q), vmem(BF, NX, NY, CH, Q),
            vmem(F32, 3, mine, FFL), vmem(BF, 3, mine, FFL), vmem(BF, NX, NY, CH, Q),
            vmem(BF, NY, CH, Q), vmem(BF, 2, NY, CH, Q), vmem(BF, NY, CH, Q), vmem(BF, NY, CH, Q),
            vmem(BF, NC, 128, Q), vmem(BF, 128, Q), vmem(F32, 128, Q),
            vmem(BF, NZH, NZL, 2 * TOK, 256), vmem(BF, 16, 2 * TOK, 256),
            dma(14), dma(3), dma(hops), dma(hops), dma(NY), dma(NY), dma(2, NY), dma(2, NY), dma(NY), dma(NY),
            dma(2, NY), dma(2, NY), dma(2, 2, NY), dma(2, 2, NY), dma(2, NY), dma(2, NY), dma(2), dma(2),
            dma(NZH, NZL), dma(16),
        ],
        compiler_params=pltpu.CompilerParams(
            collective_id=0, has_side_effects=True, vmem_limit_bytes=60 * 1024 * 1024
        ),
        name="routed_experts",
    )(tokens_a, cotangent_b, routes_a.T, routes_b.T, gates_a.T, gates_b.T,
      gate_weight, up_weight, down_weight, saved_gate, saved_up)
    return both[:TOK], both[TOK:]


def solution(mesh):
    placed = (
        P("expert", None), P("expert", None), P("expert", None),
        P("expert", None), P("expert", None), P("expert", None),
        P("expert", None, "section"), P("expert", None, "section"), P("expert", "section", None),
        P("expert", None, "section"), P("expert", None, "section"),
    )
    return jax.shard_map(
        body, mesh=mesh, in_specs=placed,
        out_specs=(P("expert", "section"), P("expert", "section")), check_vma=False,
    )
```

time: 119 us -> 113 us (0.950)
  the two profiles are of different devices: /device:TPU:1 before, /device:TPU:8 now
where the time goes in v2:
time: 113 us
  Pallas kernels  111 us (98%)
  local copies, waits for them, and re-layouts  1.32 us (1%)
    pallas_call x1, Pallas kernels, body(): pl.pallas_call(kernel, out_shape=jax.ShapeDtypeStruct((2 * TOK, COLS), BF...  111 us

profile of v2, /device:TPU:8, one launch (start us, length us, event | category | flops | bytes accessed | tf_op | source)
XLA Modules:
  0.0 112.7 jit_solution(13201586053576175813)
XLA Ops:
  0.6 110.7 %routed_experts.1 = bf16[32,224]{1,0:T(8,128)(2,1)} custom-call(bf16[16,3584]{1,0:T(8,128)(2,1)} %tok_a.1, bf16[16,3584]{1,0:T(8,128)(2,1)} %tok_b.1, s32[8,16]{1,0:T(8,128)} %bitcast.4, s32[8,16]{1,0:T(8,128)} %bitcast.5, f32[8,16]{1,0:T(8,128)} %bitcast.6, f32[8,16]{1,0:T(8,128)} %bitcast.7, bf16[1,3584,128]{2,1,0:T(8,128)(2,1)} %w_gate.1, ...), custom_call_target="tpu_custom_call" | custom-call | tf_op jit(solution)/shard_map/routed_experts/pallas_call | solution.py:404
  111.4 1.3 %fusion = (bf16[16,224]{1,0:T(8,128)(2,1)}, bf16[16,224]{1,0:T(8,128)(2,1)}) fusion(bf16[32,224]{1,0:T(8,128)(2,1)} %routed_experts.1), kind=kLoop, calls=%fused_computation | loop fusion | bytes 28672 | tf_op jit(solution)/shard_map/slice | solution.py:428

commit v3 on v2

--- a/solution.py
+++ b/solution.py
@@ -19,8 +19,11 @@
 BF, F32, I32 = jnp.bfloat16, jnp.float32, jnp.int32
 NEAR = (0, 1, 7, 2, 6, 3, 5, 4)
 POS = (0, 1, 3, 5, 7, 6, 4, 2)
-CUTS = ((0, 512), (512, 384))
-TURNS = ((0, 256, 0), (128, 384, 96), (384, 384, 64), (640, 256, 32))
+CUTS = ((0, 640), (640, 256), (0, 896))
+MOVES = ((0, 0, 256), (256, 384, 384), (640, 256, 128), (768, 768, 128))
+TURNS = (((0, 256),), ((128, 128), (640, 128), (256, 128)), ((256, 384),), ((512, 128), (768, 128)))
+SHIFTS = (0, 96, 64, 32)
+WAY = 512
 HOPS = (
     [(dz, dc, kind) for dz in (1, -1) for dc in (0, 1) for kind in (2, 0, 1)]
     + [(2, dc, kind) for dc in (0, 1) for kind in (2, 0)]
@@ -60,9 +63,9 @@
     tok_a, tok_b, routes_a, routes_b, gates_a, gates_b, w_gate, w_up, w_down, sv_gate, sv_up,
     out,
     wg, wu, wd, sg, su,
-    meta, met, tok, sel_t, send_y, rows, acc, hid, part, f1, f2, red, ret, dense, other, tot, fin_src, fin,
+    meta, met, tok, sel_t, send_y, rows, acc, hid, part, f1, f2, red, ret, dense, other, tot, fin_src, fin, hop_a, hop_b,
     w_sem, own_sem, d1_s, d1_r, d2_s, d2_r, x_s, x_r, f_s, f_r,
-    a_s, a_r, b_s, b_r, c_s, c_r, e_s, e_r, z_s, z_r,
+    a_s, a_r, b_s, b_r, c_s, c_r, e_s, e_r, z_s, z_r, h_s, h_r,
 ):
     sec, exp = lax.axis_index("section"), lax.axis_index("expert")
     x, zh = lax.div(sec, NZH), lax.rem(sec, NZH)
@@ -126,8 +129,7 @@
                 gather[n].start()
     for copy in own:
         copy.start()
-    for copy in own:
-        copy.wait()
+    own[2].wait()
     for n, (_, _, kind) in enumerate(HOPS):
         if kind == 2:
             gather[n].wait_recv()
@@ -154,6 +156,8 @@
         gate_row = jnp.sum(hit * gate_t, axis=1, keepdims=True)
         picks.append((pick, jnp.where((iota((128, 1), 0) & 1) == 1, gate_row, 1.0)))
 
+    own[0].wait()
+    own[1].wait()
     for n, (_, _, kind) in enumerate(HOPS):
         if kind != 2:
             gather[n].wait_recv()
@@ -165,9 +169,20 @@
         send_y[:, slab, :] = picked[GRP:].reshape(NY - 1, GRP, Q)
 
     def y_copy(d):
-        return remote(send_y.at[d - 1], rows.at[0, POS[NY - d]], d2_s.at[d], d2_r.at[NY - d], at(dy=d))
-
-    x_copies, forwards = [], []
+        near = slice(0, WAY) if d == HALF else slice(0, Q)
+        return remote(send_y.at[d - 1, :, near], rows.at[0, POS[NY - d], :, near], d2_s.at[d], d2_r.at[NY - d], at(dy=d))
+
+    def detour():
+        return remote(send_y.at[HALF - 1, :, WAY:Q], hop_a, d2_s.at[0], h_r.at[0], at(dy=-1))
+
+    def pass_on():
+        return remote(hop_a, rows.at[0, POS[HALF], :, WAY:Q], h_s.at[0], d2_r.at[0], at(dy=-3))
+
+    x_copies, forwards, sends = [], [], []
+
+    def go(copy):
+        copy.start()
+        sends.append(copy)
 
     def x_copy(side, p):
         return remote(rows.at[0, p], rows.at[3 - 2 * side, p], x_s.at[side, p], x_r.at[side, p], at(dx=1 - 2 * side))
@@ -179,6 +194,8 @@
     def x_step(p):
         if p:
             y_copy(NY - NEAR[p]).wait_recv()
+        if NEAR[p] == HALF:
+            pass_on().wait_recv()
         for side in range(2):
             x_copies.append(x_copy(side, p))
             x_copies[-1].start()
@@ -189,7 +206,7 @@
         forwards.append(forward(p))
         forwards[-1].start()
 
-    y_copies = [y_copy(d) for d in NEAR[1:]]
+    y_copies = [y_copy(1), y_copy(7), detour()] + [y_copy(d) for d in NEAR[3:]]
     for copy in y_copies:
         copy.start()
     x_step(0)
@@ -240,20 +257,16 @@
 
     def expand(h, k):
         q = quarter(k)
-        value = dot(hid[0], wd[q]) + dot_nt(hid[1], wg[q]) + dot_nt(hid[2], wu[q])
-        part[k, h * HALF : (h + 1) * HALF] = value.astype(BF).reshape(HALF, CH, Q)
-
-    sends = []
-
-    def go(copy):
-        copy.start()
-        sends.append(copy)
+        for to, base, width in MOVES:
+            span = slice(base, base + width)
+            value = dot(hid[0], wd[q, :, span]) + dot_nt(hid[1], wg[q, span, :]) + dot_nt(hid[2], wu[q, span, :])
+            part[k, h * HALF : (h + 1) * HALF, :, to : to + width] = value.astype(BF).reshape(HALF, CH, width)
 
     def cols(s):
         return slice(CUTS[s][0], CUTS[s][0] + CUTS[s][1])
 
     def half(h):
-        return range(h * HALF, (h + 1) * HALF)
+        return reversed(range(h * HALF, (h + 1) * HALF))
 
     def first_copy(s, p):
         return remote(part.at[2, p, :, cols(s)], f1.at[p, :, cols(s)], a_s.at[s, p], a_r.at[s, p],
@@ -280,11 +293,16 @@
             go(second_copy(s, p % 2, p))
 
     def back_copy(s, d):
+        if s == 1 and d == HALF:
+            return remote(red.at[d, :, cols(s)], hop_b, c_s.at[s, d], h_r.at[1], at(dy=-1))
         return remote(red.at[d, :, cols(s)], ret.at[(NY - d) % NY, :, cols(s)],
                       c_s.at[s, d], c_r.at[s, (NY - d) % NY], at(dy=d))
 
-    def finish(s):
-        for p in reversed(range(NY)):
+    def back_pass():
+        return remote(hop_b, ret.at[HALF, :, cols(1)], h_s.at[1], c_r.at[1, HALF], at(dy=-3))
+
+    def finish(s, h):
+        for p in half(h):
             second_copy(s, 0, p).wait_recv()
             second_copy(s, 1, p).wait_recv()
             total = part[0, p, :, cols(s)].astype(F32) + f2[0, p, :, cols(s)].astype(F32)
@@ -300,8 +318,14 @@
         return remote(dense.at[1 - c, :, cols(s)], other.at[:, cols(s)], e_s.at[s], e_r.at[s], at(dc=1))
 
     def combine(s):
-        for d in range(1, NY):
-            back_copy(s, NY - d).wait_recv()
+        if s == 0:
+            for p in range(1, HALF):
+                back_copy(2, NEAR[p]).wait_recv()
+        for p in range(HALF, NY):
+            if s == 1 and NEAR[p] == HALF:
+                back_pass().wait_recv()
+            else:
+                back_copy(s, NEAR[p]).wait_recv()
         width = CUTS[s][1]
         total = jnp.zeros((256, width), F32)
         for r in range(RANKS):
@@ -318,22 +342,26 @@
     def scatter(s):
         core_copy(s).wait_recv()
         tot[:, cols(s)] = dense[c, :, cols(s)].astype(F32) + other[:, cols(s)].astype(F32)
-        for h in (2 * s, 2 * s + 1):
-            base, width, shift = TURNS[h]
-            turned = tot[:, base : base + width]
-            if shift:
-                turned = pltpu.roll(turned, width - shift, axis=1)
+        for h in (s, s + 2):
+            pieces = [tot[:, base : base + width] for base, width in TURNS[h]]
+            turned = pieces[0] if len(pieces) == 1 else jnp.concatenate(pieces, axis=1)
+            if SHIFTS[h]:
+                turned = pltpu.roll(turned, turned.shape[1] - SHIFTS[h], axis=1)
             fin_src[h] = turned[:, 0:256].astype(BF).reshape(NZL, 2 * TOK, 256)
-        for h in (2 * s, 2 * s + 1):
-            for l in range(NZL):
-                @pl.when(z != h * NZL + l)
-                def _():
-                    z_copy(h, l).start()
-
-    for p in range(HALF + 1):
-        if p:
-            x_step(p)
-            x_forward(p - 1)
+        for j in range(8):
+            h = s + 2 * lax.rem(lax.div(zh, 2) + 1 + j // NZL, 2)
+            l = lax.rem(zl + 2 + j, NZL)
+
+            @pl.when(z != h * NZL + l)
+            def _():
+                z_copy(h, l).start()
+
+    for p in range(1, HALF + 1):
+        x_step(p)
+        x_forward(p - 1)
+        if p == 2:
+            detour().wait_recv()
+            go(pass_on())
     for k in (0, 3, 1):
         project(0, k)
     for p in (5, 6):
@@ -344,14 +372,14 @@
     project(0, 2)
     activate(0)
     expand(0, 2)
-    send_first(0, 0)
+    send_first(2, 0)
     for k in (1, 3):
         expand(0, k)
-    send_plain(0, 0)
+    send_plain(2, 0)
     x_step(7)
     x_forward(6)
     project(1, 0)
-    send_added(0, 0)
+    send_added(2, 0)
     expand(0, 0)
     x_forward(7)
     for k in (3, 1):
@@ -365,18 +393,18 @@
     for k in (1, 3):
         expand(1, k)
     send_plain(0, 1)
-    send_first(1, 0)
+    send_first(1, 1)
+    finish(2, 0)
     send_added(0, 1)
-    send_first(1, 1)
-    for h in range(2):
-        send_plain(1, h)
+    send_plain(1, 1)
     expand(1, 0)
-    for h in range(2):
-        send_added(1, h)
-    finish(0)
+    send_added(1, 1)
+    finish(0, 1)
+    finish(1, 1)
+    back_copy(1, HALF).wait_recv()
+    go(back_pass())
     combine(0)
     scatter(0)
-    finish(1)
     combine(1)
     scatter(1)
 
@@ -414,10 +442,10 @@
             vmem(F32, 3, mine, FFL), vmem(BF, 3, mine, FFL), vmem(BF, NX, NY, CH, Q),
             vmem(BF, NY, CH, Q), vmem(BF, 2, NY, CH, Q), vmem(BF, NY, CH, Q), vmem(BF, NY, CH, Q),
             vmem(BF, NC, 128, Q), vmem(BF, 128, Q), vmem(F32, 128, Q),
-            vmem(BF, NZH, NZL, 2 * TOK, 256), vmem(BF, 16, 2 * TOK, 256),
+            vmem(BF, NZH, NZL, 2 * TOK, 256), vmem(BF, 16, 2 * TOK, 256), vmem(BF, CH, Q - WAY), vmem(BF, CH, 256),
             dma(14), dma(3), dma(hops), dma(hops), dma(NY), dma(NY), dma(2, NY), dma(2, NY), dma(NY), dma(NY),
-            dma(2, NY), dma(2, NY), dma(2, 2, NY), dma(2, 2, NY), dma(2, NY), dma(2, NY), dma(2), dma(2),
-            dma(NZH, NZL), dma(16),
+            dma(3, NY), dma(3, NY), dma(3, 2, NY), dma(3, 2, NY), dma(3, NY), dma(3, NY), dma(2), dma(2),
+            dma(NZH, NZL), dma(16), dma(2), dma(2),
         ],
         compiler_params=pltpu.CompilerParams(
             collective_id=0, has_side_effects=True, vmem_limit_bytes=60 * 1024 * 1024

time: 113 us -> 110 us (0.973)
  the two profiles are of different devices: /device:TPU:8 before, /device:TPU:1 now
where the time goes in v3:
time: 110 us
  Pallas kernels  108 us (98%)
  local copies, waits for them, and re-layouts  1.32 us (1%)
    pallas_call x1, Pallas kernels, body(): pl.pallas_call(kernel, out_shape=jax.ShapeDtypeStruct((2 * TOK, COLS), BF...  108 us

profile of v3, /device:TPU:1, one launch (start us, length us, event | category | flops | bytes accessed | tf_op | source)
XLA Modules:
  0.0 110.1 jit_solution(7004064044944402323)
XLA Ops:
  0.6 108.2 %routed_experts.1 = bf16[32,224]{1,0:T(8,128)(2,1)} custom-call(bf16[16,3584]{1,0:T(8,128)(2,1)} %tok_a.1, bf16[16,3584]{1,0:T(8,128)(2,1)} %tok_b.1, s32[8,16]{1,0:T(8,128)} %bitcast.4, s32[8,16]{1,0:T(8,128)} %bitcast.5, f32[8,16]{1,0:T(8,128)} %bitcast.6, f32[8,16]{1,0:T(8,128)} %bitcast.7, bf16[1,3584,128]{2,1,0:T(8,128)(2,1)} %w_gate.1, ...), custom_call_target="tpu_custom_call" | custom-call | tf_op jit(solution)/shard_map/routed_experts/pallas_call | solution.py:432
  108.8 1.3 %fusion = (bf16[16,224]{1,0:T(8,128)(2,1)}, bf16[16,224]{1,0:T(8,128)(2,1)}) fusion(bf16[32,224]{1,0:T(8,128)(2,1)} %routed_experts.1), kind=kLoop, calls=%fused_computation | loop fusion | bytes 28672 | tf_op jit(solution)/shard_map/slice | solution.py:456

commit v4 on v3

--- a/solution.py
+++ b/solution.py
@@ -60,12 +60,12 @@
 
 
 def kernel(
-    tok_a, tok_b, routes_a, routes_b, gates_a, gates_b, w_gate, w_up, w_down, sv_gate, sv_up,
+    tok_a, tok_b, far_ra, far_rb, far_ga, far_gb, w_gate, w_up, w_down, sv_gate, sv_up,
     out,
     wg, wu, wd, sg, su,
-    meta, met, tok, sel_t, send_y, rows, acc, hid, part, f1, f2, red, ret, dense, other, tot, fin_src, fin, hop_a, hop_b,
+    meta, met, tok, sel_t, send_y, rows, acc, hid, part, f1, f2, red, ret, dense, other, tot, fin_src, fin, hop_a, hop_b, routes_a, routes_b, gates_a, gates_b,
     w_sem, own_sem, d1_s, d1_r, d2_s, d2_r, x_s, x_r, f_s, f_r,
-    a_s, a_r, b_s, b_r, c_s, c_r, e_s, e_r, z_s, z_r, h_s, h_r,
+    a_s, a_r, b_s, b_r, c_s, c_r, e_s, e_r, z_s, z_r, h_s, h_r, t_sem,
 ):
     sec, exp = lax.axis_index("section"), lax.axis_index("expert")
     x, zh = lax.div(sec, NZH), lax.rem(sec, NZH)
@@ -90,6 +90,10 @@
     for peer in peers:
         pl.semaphore_signal(barrier, inc=1, device_id=peer, device_id_type=pl.DeviceIdType.MESH)
 
+    tables = [pltpu.make_async_copy(src, dst, t_sem.at[n]) for n, (src, dst) in enumerate(
+        ((far_ra, routes_a), (far_rb, routes_b), (far_ga, gates_a), (far_gb, gates_b)))]
+    for copy in tables:
+        copy.start()
     loads = [pltpu.make_async_copy(sv_gate.at[0], sg, w_sem.at[0]),
              pltpu.make_async_copy(sv_up.at[0], su, w_sem.at[1])]
     for q in range(NX):
@@ -100,6 +104,8 @@
     for load in loads:
         load.start()
 
+    for copy in tables:
+        copy.wait()
     meta[...] = jnp.zeros((8, TOK * TOP), F32)
     meta[0:1, :] = flatten_routes(routes_a[...].astype(F32))
     meta[1:2, :] = flatten_routes(routes_b[...].astype(F32))
@@ -364,7 +370,7 @@
             go(pass_on())
     for k in (0, 3, 1):
         project(0, k)
-    for p in (5, 6):
+    for p in (5, 6, 7):
         x_step(p)
         x_forward(p - 1)
     for p in half(0):
@@ -375,15 +381,12 @@
     send_first(2, 0)
     for k in (1, 3):
         expand(0, k)
+    x_forward(7)
     send_plain(2, 0)
-    x_step(7)
-    x_forward(6)
-    project(1, 0)
+    for k in (0, 3, 1):
+        project(1, k)
     send_added(2, 0)
     expand(0, 0)
-    x_forward(7)
-    for k in (3, 1):
-        project(1, k)
     for p in half(1):
         forward(p).wait_recv()
     project(1, 2)
@@ -432,7 +435,7 @@
     both = pl.pallas_call(
         kernel,
         out_shape=jax.ShapeDtypeStruct((2 * TOK, COLS), BF),
-        in_specs=[far, far, near, near, near, near, far, far, far, far, far],
+        in_specs=[far, far, far, far, far, far, far, far, far, far, far],
         out_specs=near,
         scratch_shapes=[
             vmem(BF, NX, Q, FFL), vmem(BF, NX, Q, FFL), vmem(BF, NX, FFL, Q),
@@ -443,9 +446,10 @@
             vmem(BF, NY, CH, Q), vmem(BF, 2, NY, CH, Q), vmem(BF, NY, CH, Q), vmem(BF, NY, CH, Q),
             vmem(BF, NC, 128, Q), vmem(BF, 128, Q), vmem(F32, 128, Q),
             vmem(BF, NZH, NZL, 2 * TOK, 256), vmem(BF, 16, 2 * TOK, 256), vmem(BF, CH, Q - WAY), vmem(BF, CH, 256),
+            vmem(I32, TOP, TOK), vmem(I32, TOP, TOK), vmem(F32, TOP, TOK), vmem(F32, TOP, TOK),
             dma(14), dma(3), dma(hops), dma(hops), dma(NY), dma(NY), dma(2, NY), dma(2, NY), dma(NY), dma(NY),
             dma(3, NY), dma(3, NY), dma(3, 2, NY), dma(3, 2, NY), dma(3, NY), dma(3, NY), dma(2), dma(2),
-            dma(NZH, NZL), dma(16), dma(2), dma(2),
+            dma(NZH, NZL), dma(16), dma(2), dma(2), dma(4),
         ],
         compiler_params=pltpu.CompilerParams(
             collective_id=0, has_side_effects=True, vmem_limit_bytes=60 * 1024 * 1024

time: 110 us -> 110 us (level)
  no operation moved by 1% of the time
where the time goes in v4:
time: 110 us
  Pallas kernels  108 us (98%)
  local copies, waits for them, and re-layouts  1.32 us (1%)
    pallas_call x1, Pallas kernels, body(): pl.pallas_call(kernel, out_shape=jax.ShapeDtypeStruct((2 * TOK, COLS), BF...  108 us

profile of v4, /device:TPU:1, one launch (start us, length us, event | category | flops | bytes accessed | tf_op | source)
XLA Modules:
  0.0 109.8 jit_solution(10599283328960847951)
XLA Ops:
  0.6 107.8 %routed_experts.1 = bf16[32,224]{1,0:T(8,128)(2,1)} custom-call(bf16[16,3584]{1,0:T(8,128)(2,1)} %tok_a.1, bf16[16,3584]{1,0:T(8,128)(2,1)} %tok_b.1, s32[8,16]{1,0:T(8,128)} %bitcast.4, s32[8,16]{1,0:T(8,128)} %bitcast.5, f32[8,16]{1,0:T(8,128)} %bitcast.6, f32[8,16]{1,0:T(8,128)} %bitcast.7, bf16[1,3584,128]{2,1,0:T(8,128)(2,1)} %w_gate.1, ...), custom_call_target="tpu_custom_call" | custom-call | tf_op jit(solution)/shard_map/routed_experts/pallas_call | solution.py:435
  108.5 1.3 %fusion = (bf16[16,224]{1,0:T(8,128)(2,1)}, bf16[16,224]{1,0:T(8,128)(2,1)}) fusion(bf16[32,224]{1,0:T(8,128)(2,1)} %routed_experts.1), kind=kLoop, calls=%fused_computation | loop fusion | bytes 28672 | tf_op jit(solution)/shard_map/slice | solution.py:460
